TPU v7x, 32 devices: a whole 2x2x4 slice. The times are simulated.
32 devices in a mesh: role: 2 (over y), space: 4 (over z), freq: 4 (over x, core).
Axes of the slice: x: 2, y: 2, z: 4, core: 2. Of those that a mesh axis runs over, the one named last changes fastest.
Arguments:
- fields: float32 [2, 5, 8, 512], P('role', None, 'freq', 'space'), may hold values from -6 to 6
- spectra: float32 [2, 128, 4, 8, 512], P('role', 'freq', None, None, 'space'), may hold values from -6 to 6
- freq_index: int32 [128], P('freq'), may hold values from 1 to 63
- freq_weight: float32 [128], P('freq'), may hold values from 0.5 to 2
- material_ids: int32 [8, 512], P('freq', 'space'), may hold values from 0 to 7
- material: float32 [3, 8], replicated, may hold values from 0.5 to 2
- source_cells: int32 [2, 16], P('role'), may hold values from 0 to 4095
- wavelets: float32 [2, 8, 16], P('role'), may hold values from -6 to 6
Outputs:
- fields_out: float32 [2, 5, 8, 512], P('role', None, 'freq', 'space')
- spectra_out: float32 [2, 128, 4, 8, 512], P('role', 'freq', None, None, 'space')
- gradient: float32 [8, 512], P(('role', 'freq'), 'space')
Inputs may be any that keep to these rules, and one draw needn't show every extreme that they name: `source_cells`: cells may repeat.
All inputs are finite; a program needn't handle non-finite values.
Results may differ from a plain program's by a relative error of at most 0.0033.
Values may be sent and summed in bfloat16 or wider, within the bound.
A program may use at most 64 MiB of HBM per device.

v0:
```python
import functools
import math

import jax
import jax.numpy as jnp
from jax import lax
from jax.experimental import pallas as pl
from jax.experimental.pallas import tpu as pltpu
from jax.sharding import PartitionSpec as P

STEPS = 8
PERIOD = 64
COURANT = 0.18
TWO_PI = 6.283185307179586
PLANES = 6
MESH = pl.DeviceIdType.MESH


def log2(n):
    bits = n.bit_length() - 1
    assert n == 1 << bits
    return bits


def kernel(
    sizes,
    fields, ids, freq_index, freq_weight, material, cells, wavelets, spectra,
    fields_out, spectra_out, gradient,
    block, packed, center, halo, cells_far, wavelets_far, planes, edges,
    inject_left, inject, table, snaps, spectrum, bulk, bulk_far, final, sums, sums_far,
    center_send, center_recv, halo_send, halo_recv, small_send, small_recv,
    bulk_send, bulk_recv, sums_send, sums_recv, load_sem, store_sem,
):
    groups, spaces, local_freqs, rows, columns = sizes
    count = 2 * groups
    rows_all = rows * groups
    span = 2 * STEPS
    wide = 2 * columns
    half = local_freqs // 2
    nmat = material.shape[1]
    nsrc = cells.shape[1]
    role = lax.axis_index("role")
    space = lax.axis_index("space")
    group = lax.axis_index("freq")
    other = 1 - role
    me = role * groups + group

    def device(index, at):
        return {"role": index // groups, "space": at, "freq": index % groups}

    def peer(step):
        return lax.rem(me + step, count)

    has_low = space > 0
    has_high = space < spaces - 1

    halo[...] = jnp.zeros_like(halo)

    barrier = pltpu.get_barrier_semaphore()

    @pl.when(has_low)
    def _():
        for step in range(count):
            pl.semaphore_signal(barrier, inc=1, device_id=device(peer(step), space - 1), device_id_type=MESH)

    @pl.when(has_high)
    def _():
        for step in range(count):
            pl.semaphore_signal(barrier, inc=1, device_id=device(peer(step), space + 1), device_id_type=MESH)

    for step in range(1, count):
        pl.semaphore_signal(barrier, inc=1, device_id=device(peer(step), space), device_id_type=MESH)

    away = pl.ds(other * half, half)
    home = pl.ds(role * half, half)
    load_away = pltpu.make_async_copy(spectra.at[0, away], spectrum.at[away], load_sem.at[0])
    load_home = pltpu.make_async_copy(spectra.at[0, home], spectrum.at[home], load_sem.at[1])
    load_away.start()
    load_home.start()

    for plane in range(PLANES - 1):
        block[plane] = fields[0, plane]
    block[PLANES - 1] = (ids[...] + 1).astype(jnp.float32)
    lane = lax.broadcasted_iota(jnp.int32, (rows, columns), 1)
    pack = jnp.zeros((rows, columns), jnp.float32)
    for plane in range(PLANES):
        value = block[plane]
        if plane:
            value = pltpu.roll(value, span * plane, 1)
        place = (lane - (span * plane - STEPS)) & (columns - 1)
        pack = jnp.where(place < span, value, pack)
    packed[...] = pack

    beside = lax.div(space + spaces - 1, spaces) + lax.div(2 * spaces - 2 - space, spaces)
    pl.semaphore_wait(barrier, count - 1 + count * beside)

    def halo_copy(side, step, at, slot):
        return pltpu.make_async_remote_copy(
            src_ref=packed, dst_ref=halo.at[side, slot],
            send_sem=halo_send.at[side, step], recv_sem=halo_recv.at[side, slot],
            device_id=device(peer(step), at), device_id_type=MESH,
        )

    def center_copy(step, slot):
        return pltpu.make_async_remote_copy(
            src_ref=block, dst_ref=center.at[slot],
            send_sem=center_send.at[step], recv_sem=center_recv.at[slot],
            device_id=device(peer(step), space), device_id_type=MESH,
        )

    partner = {"role": other, "space": space, "freq": group}
    cells_copy = pltpu.make_async_remote_copy(
        src_ref=cells, dst_ref=cells_far, send_sem=small_send.at[0], recv_sem=small_recv.at[0],
        device_id=partner, device_id_type=MESH,
    )
    wavelets_copy = pltpu.make_async_remote_copy(
        src_ref=wavelets, dst_ref=wavelets_far, send_sem=small_send.at[1], recv_sem=small_recv.at[1],
        device_id=partner, device_id_type=MESH,
    )
    bulk_copy = pltpu.make_async_remote_copy(
        src_ref=bulk, dst_ref=bulk_far, send_sem=bulk_send, recv_sem=bulk_recv,
        device_id=partner, device_id_type=MESH,
    )

    @pl.when(has_high)
    def _():
        for step in range(count):
            halo_copy(0, step, space + 1, me).start()

    @pl.when(has_low)
    def _():
        for step in range(count):
            halo_copy(1, step, space - 1, me).start()

    for step in range(1, count):
        center_copy(step, me).start()
    cells_copy.start()
    wavelets_copy.start()

    load_away.wait()
    for index in range(half):
        bulk[index] = spectrum[other * half + index].reshape(4 * rows_all, columns).astype(jnp.bfloat16)
    bulk_copy.start()

    depth = 2 * STEPS * rows_all
    at_row = lax.broadcasted_iota(jnp.int32, (2 * rows_all, depth), 0)
    at_lane = lax.broadcasted_iota(jnp.int32, (2 * rows_all, depth), 1)
    step_of = (at_lane >> log2(rows_all)) & (STEPS - 1)
    turn = jnp.where(at_lane >= STEPS * rows_all, PERIOD // 4, 0)
    match = (at_lane & (rows_all - 1)) == (at_row & (rows_all - 1))
    for pair in range(local_freqs // 2):
        number = jnp.where(at_row < rows_all, freq_index[2 * pair], freq_index[2 * pair + 1])
        turns = (number * step_of + turn) & (PERIOD - 1)
        value = jnp.cos(turns.astype(jnp.float32) * (TWO_PI / PERIOD))
        table[pl.ds(pair * 2 * rows_all, 2 * rows_all), :] = jnp.where(match, value, 0.0).astype(jnp.bfloat16)

    def injection(which, cell_row, wavelet_rows):
        cell_at = jnp.broadcast_to(cell_row, (rows_all, nsrc)) >> log2(columns * spaces)
        row_at = lax.broadcasted_iota(jnp.int32, (rows_all, nsrc), 0)
        for tick in range(STEPS):
            amount = jnp.broadcast_to(wavelet_rows[tick:tick + 1, :], (rows_all, nsrc))
            inject_left[pl.ds(tick * rows_all, rows_all), :] = jnp.where(cell_at == row_at, amount, 0.0)
        column_at = lax.broadcasted_iota(jnp.int32, (wide, nsrc), 0)
        shift = jnp.where(column_at >= wide - STEPS, column_at - wide, column_at) + space * columns
        shift = jnp.where((column_at >= columns + STEPS) & (column_at < wide - STEPS), -1, shift)
        wanted = jnp.broadcast_to(cell_row, (wide, nsrc)) & (columns * spaces - 1)
        hit = (shift == wanted).astype(jnp.float32)
        inject[which] = lax.dot_general(
            inject_left[...], hit, (((1,), (1,)), ((), ())),
            precision=lax.Precision.HIGHEST, preferred_element_type=jnp.float32,
        )

    injection(0, cells[...], wavelets[0])

    cells_copy.wait_recv()
    wavelets_copy.wait_recv()
    injection(1, cells_far[...], wavelets_far[0])

    for step in range(1, count):
        center_copy(step, peer(step)).wait_recv()
    for plane in range(PLANES):
        center[me, plane] = block[plane]

    for which, owner in ((0, role), (1, other)):
        for part in range(groups):
            slot = owner * groups + part
            for plane in range(PLANES):
                planes[which, plane, pl.ds(part * rows, rows), :] = center[slot, plane]

    @pl.when(has_low)
    def _():
        for step in range(count):
            halo_copy(0, step, space - 1, peer(step)).wait_recv()

    @pl.when(has_high)
    def _():
        for step in range(count):
            halo_copy(1, step, space + 1, peer(step)).wait_recv()

    low_part = (lane & (span - 1)) < STEPS
    for which, owner in ((0, role), (1, other)):
        for part in range(groups):
            slot = owner * groups + part
            edges[which, pl.ds(part * rows, rows), :] = jnp.where(low_part, halo[1, slot], halo[0, slot])

    lane_all = lax.broadcasted_iota(jnp.int32, (rows_all, columns), 1)
    rim = (lane_all < STEPS) | (lane_all >= columns - STEPS)

    def whole(which, plane):
        outer = edges[which]
        if plane:
            outer = pltpu.roll(outer, columns - span * plane, 1)
        return jnp.concatenate([planes[which, plane], jnp.where(rim, outer, 0.0)], axis=1)

    ident = whole(0, PLANES - 1)
    props = [jnp.zeros_like(ident) for _ in range(3)]
    for block_id in range(nmat):
        same = ident == float(block_id + 1)
        props = [jnp.where(same, material[k, block_id], props[k]) for k in range(3)]
    buoyancy = COURANT * props[0]
    first = COURANT * props[1]
    second = COURANT * props[2]
    stiff = first + 2.0 * second

    row_id = lax.broadcasted_iota(jnp.int32, (rows_all, wide), 0)
    not_top = row_id > 0
    not_end = row_id < rows_all - 1

    def up(x):
        return jnp.where(not_end, pltpu.roll(x, rows_all - 1, 0), 0.0)

    def down(x):
        return jnp.where(not_top, pltpu.roll(x, 1, 0), 0.0)

    def right(x):
        return pltpu.roll(x, wide - 1, 1)

    def left(x):
        return pltpu.roll(x, 1, 1)

    state = [[whole(which, plane) for plane in range(5)] for which in range(2)]
    for tick in range(STEPS):
        at = pl.ds(tick * rows_all, rows_all)
        for which in range(2):
            vx, vz, xx, zz, xz = state[which]
            vx = vx + buoyancy * ((up(xx) - xx) + (xz - left(xz)))
            vz = vz + buoyancy * ((xz - down(xz)) + (right(zz) - zz))
            source = inject[which, at, :]
            ex = vx - down(vx)
            ez = vz - left(vz)
            xx = xx + (stiff * ex + first * ez) + source
            zz = zz + (first * ex + stiff * ez) + source
            xz = xz + second * ((right(vx) - vx) + (up(vz) - vz))
            state[which] = [vx, vz, xx, zz, xz]
            snaps[which, at, 0:columns] = vx[:, :columns]
            snaps[which, at, columns:wide] = vz[:, :columns]
    for plane in range(5):
        final[plane] = state[0][plane][:, :columns]
    for plane in range(5):
        fields_out[0, plane] = final[plane, pl.ds(group * rows, rows), :]

    def right_side(which):
        snap = snaps[which].astype(jnp.bfloat16)
        zero = jnp.zeros_like(snap)
        return jnp.concatenate(
            [jnp.concatenate([snap, zero], axis=1), jnp.concatenate([zero, snap], axis=1)], axis=0
        )

    def products(which_freqs, side):
        lines = pl.ds(pl.multiple_of(which_freqs * half * rows_all, 16), half * rows_all)
        return jnp.dot(table[lines, :], side, preferred_element_type=jnp.float32)

    def piece(value, index, part):
        return value[index * rows_all:(index + 1) * rows_all, part * columns:(part + 1) * columns]

    load_home.wait()
    side = right_side(0)
    near = products(role, side)
    far = products(role, right_side(1))
    bulk_copy.wait_recv()
    total = jnp.zeros((rows_all, columns), jnp.float32)
    for index in range(half):
        theirs = bulk_far[index].astype(jnp.float32)
        term = jnp.zeros((rows_all, columns), jnp.float32)
        for part in range(4):
            mine = spectrum[role * half + index, part] + piece(near, index, part)
            spectrum[role * half + index, part] = mine
            term = term + mine * (theirs[part * rows_all:(part + 1) * rows_all] + piece(far, index, part))
        total = total + freq_weight[role * half + index] * term
    total = total * (1.0 / (local_freqs * groups))
    each = rows_all // count
    for slot in range(count):
        sums[slot] = total[slot * each:(slot + 1) * each]

    def sums_copy(step, slot):
        return pltpu.make_async_remote_copy(
            src_ref=sums.at[peer(step)], dst_ref=sums_far.at[slot],
            send_sem=sums_send.at[step], recv_sem=sums_recv.at[slot],
            device_id=device(peer(step), space), device_id_type=MESH,
        )

    for step in range(1, count):
        sums_copy(step, me).start()
    store_home = pltpu.make_async_copy(spectrum.at[home], spectra_out.at[0, home], store_sem.at[0])
    store_home.start()

    rest = products(other, side)
    for index in range(half):
        for part in range(4):
            spectrum[other * half + index, part] = spectrum[other * half + index, part] + piece(rest, index, part)
    store_away = pltpu.make_async_copy(spectrum.at[away], spectra_out.at[0, away], store_sem.at[1])
    store_away.start()

    answer = sums[me]
    for step in range(1, count):
        sums_copy(step, peer(step)).wait_recv()
        answer = answer + sums_far[peer(step)]
    gradient[...] = answer

    @pl.when(has_high)
    def _():
        for step in range(count):
            halo_copy(0, step, space + 1, me).wait_send()

    @pl.when(has_low)
    def _():
        for step in range(count):
            halo_copy(1, step, space - 1, me).wait_send()

    for step in range(1, count):
        center_copy(step, me).wait_send()
        sums_copy(step, me).wait_send()
    cells_copy.wait_send()
    wavelets_copy.wait_send()
    bulk_copy.wait_send()
    store_home.wait()
    store_away.wait()


def local(fields, spectra, freq_index, freq_weight, material_ids, material, source_cells, wavelets):
    groups = lax.axis_size("freq")
    spaces = lax.axis_size("space")
    rows, columns = fields.shape[2:]
    local_freqs = freq_index.shape[0]
    rows_all = rows * groups
    count = 2 * groups
    half = local_freqs // 2
    nsrc = source_cells.shape[1]
    wide = 2 * columns
    sizes = (groups, spaces, local_freqs, rows, columns)
    f32 = jnp.float32
    vmem = pl.BlockSpec(memory_space=pltpu.VMEM)
    smem = pl.BlockSpec(memory_space=pltpu.SMEM)
    anywhere = pl.BlockSpec(memory_space=pl.ANY)
    dma = pltpu.SemaphoreType.DMA
    return tuple(pl.pallas_call(
        functools.partial(kernel, sizes),
        out_shape=(
            jax.ShapeDtypeStruct(fields.shape, f32),
            jax.ShapeDtypeStruct(spectra.shape, f32),
            jax.ShapeDtypeStruct((rows_all // count, columns), f32),
        ),
        in_specs=[vmem, vmem, smem, smem, smem, vmem, vmem, anywhere],
        out_specs=(vmem, anywhere, vmem),
        scratch_shapes=[
            pltpu.VMEM((PLANES, rows, columns), f32),
            pltpu.VMEM((rows, columns), f32),
            pltpu.VMEM((count, PLANES, rows, columns), f32),
            pltpu.VMEM((2, count, rows, columns), f32),
            pltpu.VMEM((1, nsrc), jnp.int32),
            pltpu.VMEM((1, STEPS, nsrc), f32),
            pltpu.VMEM((2, PLANES, rows_all, columns), f32),
            pltpu.VMEM((2, rows_all, columns), f32),
            pltpu.VMEM((STEPS * rows_all, nsrc), f32),
            pltpu.VMEM((2, STEPS * rows_all, wide), f32),
            pltpu.VMEM((local_freqs * rows_all, 2 * STEPS * rows_all), jnp.bfloat16),
            pltpu.VMEM((2, STEPS * rows_all, wide), f32),
            pltpu.VMEM((local_freqs, 4, rows_all, columns), f32),
            pltpu.VMEM((half, 4 * rows_all, columns), jnp.bfloat16),
            pltpu.VMEM((half, 4 * rows_all, columns), jnp.bfloat16),
            pltpu.VMEM((5, rows_all, columns), f32),
            pltpu.VMEM((count, rows_all // count, columns), f32),
            pltpu.VMEM((count, rows_all // count, columns), f32),
            dma((count,)), dma((count,)), dma((2, count)), dma((2, count)), dma((2,)), dma((2,)),
            dma, dma, dma((count,)), dma((count,)), dma((2,)), dma((2,)),
        ],
        compiler_params=pltpu.CompilerParams(collective_id=0, has_side_effects=True),
    )(fields, material_ids, freq_index, freq_weight, material, source_cells, wavelets, spectra))


def solution(mesh):
    return jax.shard_map(
        local,
        mesh=mesh,
        in_specs=(
            P("role", None, "freq", "space"),
            P("role", "freq", None, None, "space"),
            P("freq"),
            P("freq"),
            P("freq", "space"),
            P(),
            P("role", None),
            P("role", None, None),
        ),
        out_specs=(
            P("role", None, "freq", "space"),
            P("role", "freq", None, None, "space"),
            P(("role", "freq"), "space"),
        ),
        check_vma=False,
    )
```

profile of v0, /device:TPU:0, one launch (start us, length us, event | category | flops | bytes accessed | tf_op | source)
XLA Modules:
  0.0 20.1 jit_solution(4037982945683303433)
XLA Ops:
  0.6 15.8 %shard_map.103 = (f32[1,5,2,128]{3,2,1,0:T(2,128)}, f32[1,32,4,8,128]{4,3,2,1,0:T(8,128)}, f32[1,128]{1,0:T(1,128)}) custom-call(f32[1,5,2,128]{3,2,1,0:T(2,128)} %fields.1, s32[2,128]{1,0:T(2,128)} %ids.1, s32[32]{0:T(128)} %freq_index.1, f32[32]{0:T(128)} %freq_weight.1, f32[3,8]{1,0:T(4,128)} %material.1, s32[1,16]{1,0:T(1,128)} %cells.1, ...), custom_call_target="tpu_custom_call" | custom-call | tf_op jit(solution)/shard_map/pallas_call | solution.py:356
  16.4 0.0 copy-start
  16.5 0.7 %copy-done = f32[1,5,2,128]{3,2,1,0:T(2,128)S(1)} copy-done((f32[1,5,2,128]{3,2,1,0:T(2,128)S(1)}, f32[1,5,2,128]{3,2,1,0:T(2,128)}, u32[]{:S(2)}) %copy-start) | copy-done | bytes 5144
  17.1 0.6 %copy.14 = f32[1,5,2,128]{3,2,1,0:T(2,128)} copy(f32[1,5,2,128]{3,2,1,0:T(2,128)S(1)} %copy-done) | data formatting | bytes 10240
  17.7 0.0 copy-start.1
  17.7 1.9 %copy.15 = f32[1,32,4,8,128]{4,3,2,1,0:T(8,128)} copy(f32[1,32,4,8,128]{4,3,2,1,0:T(8,128)} %get-tuple-element.7) | data formatting | bytes 1048576
  19.6 0.0 copy-done.1
  19.6 0.5 %copy.16 = f32[1,128]{1,0:T(1,128)} copy(f32[1,128]{1,0:T(1,128)S(1)} %copy-done.1) | data formatting | bytes 1024
Async XLA Ops:
  16.4 0.7 %copy-start = (f32[1,5,2,128]{3,2,1,0:T(2,128)S(1)}, f32[1,5,2,128]{3,2,1,0:T(2,128)}, u32[]{:S(2)}) copy-start(f32[1,5,2,128]{3,2,1,0:T(2,128)} %get-tuple-element.6) | copy-start | bytes 15364
  17.7 1.9 %copy-start.1 = (f32[1,128]{1,0:T(1,128)S(1)}, f32[1,128]{1,0:T(1,128)}, u32[]{:S(2)}) copy-start(f32[1,128]{1,0:T(1,128)} %get-tuple-element.8) | copy-start | bytes 1540
where the time goes:
time: 20.3 us; the launch traced here: 20.1 us
  Pallas kernels  15.8 us (78%)
  local copies, waits for them, and re-layouts  3.66 us (18%)
  between operations  0.65 us (3%)
    pallas_call x1, Pallas kernels, local(): pl.pallas_call(functools.partial(kernel, sizes), out_shape=(jax.ShapeDtyp...  15.8 us
    unnamed x7, local copies, waits for them, and re-layouts  3.66 us

commit v1 on v0

--- a/solution.py
+++ b/solution.py
@@ -25,11 +25,11 @@
 def kernel(
     sizes,
     fields, ids, freq_index, freq_weight, material, cells, wavelets, spectra,
-    fields_out, spectra_out, gradient,
+    fields_out, spectrum, gradient,
     block, packed, center, halo, cells_far, wavelets_far, planes, edges,
-    inject_left, inject, table, snaps, spectrum, bulk, bulk_far, final, sums, sums_far,
+    inject_left, inject, table, snaps, bulk, bulk_far, final, sums, sums_far,
     center_send, center_recv, halo_send, halo_recv, small_send, small_recv,
-    bulk_send, bulk_recv, sums_send, sums_recv, load_sem, store_sem,
+    bulk_send, bulk_recv, sums_send, sums_recv, load_sem,
 ):
     groups, spaces, local_freqs, rows, columns = sizes
     count = 2 * groups
@@ -301,15 +301,10 @@
 
     for step in range(1, count):
         sums_copy(step, me).start()
-    store_home = pltpu.make_async_copy(spectrum.at[home], spectra_out.at[0, home], store_sem.at[0])
-    store_home.start()
-
     rest = products(other, side)
     for index in range(half):
         for part in range(4):
             spectrum[other * half + index, part] = spectrum[other * half + index, part] + piece(rest, index, part)
-    store_away = pltpu.make_async_copy(spectrum.at[away], spectra_out.at[0, away], store_sem.at[1])
-    store_away.start()
 
     answer = sums[me]
     for step in range(1, count):
@@ -333,8 +328,18 @@
     cells_copy.wait_send()
     wavelets_copy.wait_send()
     bulk_copy.wait_send()
-    store_home.wait()
-    store_away.wait()
+
+
+def deliver(fields, spectrum, gradient, fields_out, spectra_out, gradient_out, sem):
+    copies = [
+        pltpu.make_async_copy(spectrum, spectra_out.at[0], sem.at[0]),
+        pltpu.make_async_copy(fields, fields_out, sem.at[1]),
+        pltpu.make_async_copy(gradient, gradient_out, sem.at[2]),
+    ]
+    for copy in copies:
+        copy.start()
+    for copy in copies:
+        copy.wait()
 
 
 def local(fields, spectra, freq_index, freq_weight, material_ids, material, source_cells, wavelets):
@@ -353,15 +358,15 @@
     smem = pl.BlockSpec(memory_space=pltpu.SMEM)
     anywhere = pl.BlockSpec(memory_space=pl.ANY)
     dma = pltpu.SemaphoreType.DMA
-    return tuple(pl.pallas_call(
+    results = pl.pallas_call(
         functools.partial(kernel, sizes),
         out_shape=(
-            jax.ShapeDtypeStruct(fields.shape, f32),
-            jax.ShapeDtypeStruct(spectra.shape, f32),
-            jax.ShapeDtypeStruct((rows_all // count, columns), f32),
+            pltpu.VMEM(fields.shape, f32),
+            pltpu.VMEM(spectra.shape[1:], f32),
+            pltpu.VMEM((rows_all // count, columns), f32),
         ),
         in_specs=[vmem, vmem, smem, smem, smem, vmem, vmem, anywhere],
-        out_specs=(vmem, anywhere, vmem),
+        out_specs=(vmem, vmem, vmem),
         scratch_shapes=[
             pltpu.VMEM((PLANES, rows, columns), f32),
             pltpu.VMEM((rows, columns), f32),
@@ -375,17 +380,27 @@
             pltpu.VMEM((2, STEPS * rows_all, wide), f32),
             pltpu.VMEM((local_freqs * rows_all, 2 * STEPS * rows_all), jnp.bfloat16),
             pltpu.VMEM((2, STEPS * rows_all, wide), f32),
-            pltpu.VMEM((local_freqs, 4, rows_all, columns), f32),
             pltpu.VMEM((half, 4 * rows_all, columns), jnp.bfloat16),
             pltpu.VMEM((half, 4 * rows_all, columns), jnp.bfloat16),
             pltpu.VMEM((5, rows_all, columns), f32),
             pltpu.VMEM((count, rows_all // count, columns), f32),
             pltpu.VMEM((count, rows_all // count, columns), f32),
             dma((count,)), dma((count,)), dma((2, count)), dma((2, count)), dma((2,)), dma((2,)),
-            dma, dma, dma((count,)), dma((count,)), dma((2,)), dma((2,)),
+            dma, dma, dma((count,)), dma((count,)), dma((2,)),
         ],
         compiler_params=pltpu.CompilerParams(collective_id=0, has_side_effects=True),
-    )(fields, material_ids, freq_index, freq_weight, material, source_cells, wavelets, spectra))
+    )(fields, material_ids, freq_index, freq_weight, material, source_cells, wavelets, spectra)
+    return tuple(pl.pallas_call(
+        deliver,
+        out_shape=(
+            jax.ShapeDtypeStruct(fields.shape, f32),
+            jax.ShapeDtypeStruct(spectra.shape, f32),
+            jax.ShapeDtypeStruct((rows_all // count, columns), f32),
+        ),
+        in_specs=[vmem, vmem, vmem],
+        out_specs=(anywhere, anywhere, anywhere),
+        scratch_shapes=[dma((3,))],
+    )(*[pltpu.with_memory_space_constraint(x, pltpu.VMEM) for x in results]))
 
 
 def solution(mesh):

time: 20.3 us -> 16.8 us (0.83)
  local copies, waits for them, and re-layouts: 3.66 us -> 0 us
    unnamed x7 -> x0, local copies, waits for them, and re-layouts: 3.66 us -> none
    pallas_call x1 -> x2, Pallas kernels: 15.8 us -> 16 us  [the longest x1 15.2 us: local(): pl.pallas_call(functools.partial(kernel, sizes), out_shape=(pltpu.VMEM(fi...]
where the time goes in v1:
time: 16.8 us; the launch traced here: 16.7 us
  Pallas kernels  16 us (95%)
  between operations  0.64 us (4%)
    pallas_call x1, Pallas kernels, local(): pl.pallas_call(functools.partial(kernel, sizes), out_shape=(pltpu.VMEM(fi...  15.2 us
    pallas_call x1, Pallas kernels, local(): pl.pallas_call(deliver, out_shape=(jax.ShapeDtypeStruct(fields.shape, f32...  0.83 us

profile of v1, /device:TPU:0, one launch (start us, length us, event | category | flops | bytes accessed | tf_op | source)
XLA Modules:
  0.0 16.7 jit_solution(15717470541817408574)
XLA Ops:
  0.6 15.2 %shard_map.103 = (f32[1,5,2,128]{3,2,1,0:T(2,128)S(1)}, f32[32,4,8,128]{3,2,1,0:T(8,128)S(1)}, f32[1,128]{1,0:T(1,128)S(1)}) custom-call(f32[1,5,2,128]{3,2,1,0:T(2,128)} %fields.1, s32[2,128]{1,0:T(2,128)} %ids.1, s32[32]{0:T(128)} %freq_index.1, f32[32]{0:T(128)} %freq_weight.1, f32[3,8]{1,0:T(4,128)} %material.1, s32[1,16]{1,0:T(1,128)} %cells.1, ...), custom_call_target="tpu_custom_call" | custom-call | tf_op jit(solution)/shard_map/pallas_call | solution.py:361
  15.8 0.8 %shard_map.104 = (f32[1,5,2,128]{3,2,1,0:T(2,128)}, f32[1,32,4,8,128]{4,3,2,1,0:T(8,128)}, f32[1,128]{1,0:T(1,128)}) custom-call(f32[1,5,2,128]{3,2,1,0:T(2,128)S(1)} %get-tuple-element.6.fields, f32[32,4,8,128]{3,2,1,0:T(8,128)S(1)} %get-tuple-element.7.spectrum, f32[1,128]{1,0:T(1,128)S(1)} %get-tuple-element.8.gradient), custom_call_target="tpu_custom_call" | custom-call | tf_op jit(solution)/shard_map/pallas_call | solution.py:393

commit v2 on v1

--- a/solution.py
+++ b/solution.py
@@ -13,6 +13,7 @@
 COURANT = 0.18
 TWO_PI = 6.283185307179586
 PLANES = 6
+PIECES = 8
 MESH = pl.DeviceIdType.MESH
 
 
@@ -24,12 +25,13 @@
 
 def kernel(
     sizes,
-    fields, ids, freq_index, freq_weight, material, cells, wavelets, spectra,
+    fields_in, ids_in, freq_index_in, freq_weight_in, material_in, cells_in, wavelets_in, spectra,
     fields_out, spectrum, gradient,
+    ids, freq_index, freq_weight, material, cells, wavelets,
     block, packed, center, halo, cells_far, wavelets_far, planes, edges,
     inject_left, inject, table, snaps, bulk, bulk_far, final, sums, sums_far,
     center_send, center_recv, halo_send, halo_recv, small_send, small_recv,
-    bulk_send, bulk_recv, sums_send, sums_recv, load_sem,
+    bulk_send, bulk_recv, sums_send, sums_recv, load_sem, input_sem,
 ):
     groups, spaces, local_freqs, rows, columns = sizes
     count = 2 * groups
@@ -45,41 +47,59 @@
     other = 1 - role
     me = role * groups + group
 
-    def device(index, at):
-        return {"role": index // groups, "space": at, "freq": index % groups}
+    places = []
+    for flip in (role, other):
+        for step in range(groups):
+            places.append((flip, lax.rem(group + step, groups)))
+    slots = [flip * groups + at for flip, at in places]
+
+    def device(step, at):
+        return {"role": places[step][0], "space": at, "freq": places[step][1]}
 
     def peer(step):
-        return lax.rem(me + step, count)
-
-    has_low = space > 0
-    has_high = space < spaces - 1
-
-    halo[...] = jnp.zeros_like(halo)
-
-    barrier = pltpu.get_barrier_semaphore()
-
-    @pl.when(has_low)
-    def _():
-        for step in range(count):
-            pl.semaphore_signal(barrier, inc=1, device_id=device(peer(step), space - 1), device_id_type=MESH)
-
-    @pl.when(has_high)
-    def _():
-        for step in range(count):
-            pl.semaphore_signal(barrier, inc=1, device_id=device(peer(step), space + 1), device_id_type=MESH)
-
-    for step in range(1, count):
-        pl.semaphore_signal(barrier, inc=1, device_id=device(peer(step), space), device_id_type=MESH)
+        return slots[step]
 
     away = pl.ds(other * half, half)
     home = pl.ds(role * half, half)
     load_away = pltpu.make_async_copy(spectra.at[0, away], spectrum.at[away], load_sem.at[0])
     load_home = pltpu.make_async_copy(spectra.at[0, home], spectrum.at[home], load_sem.at[1])
+    inputs = [
+        pltpu.make_async_copy(source, target, input_sem.at[index])
+        for index, (source, target) in enumerate((
+            (fields_in.at[0], block.at[pl.ds(0, PLANES - 1)]), (ids_in, ids), (cells_in, cells),
+            (wavelets_in, wavelets), (freq_index_in, freq_index), (material_in, material),
+            (freq_weight_in, freq_weight),
+        ))
+    ]
+
+    has_low = space > 0
+    has_high = space < spaces - 1
+
+    for copy in inputs:
+        copy.start()
+
+    halo[...] = jnp.zeros_like(halo)
+
+    barrier = pltpu.get_barrier_semaphore()
+
+    @pl.when(has_low)
+    def _():
+        for step in range(count):
+            pl.semaphore_signal(barrier, inc=1, device_id=device(step, space - 1), device_id_type=MESH)
+
+    @pl.when(has_high)
+    def _():
+        for step in range(count):
+            pl.semaphore_signal(barrier, inc=1, device_id=device(step, space + 1), device_id_type=MESH)
+
+    for step in range(1, count):
+        pl.semaphore_signal(barrier, inc=1, device_id=device(step, space), device_id_type=MESH)
+
     load_away.start()
     load_home.start()
-
-    for plane in range(PLANES - 1):
-        block[plane] = fields[0, plane]
+    for copy in inputs[:2]:
+        copy.wait()
+
     block[PLANES - 1] = (ids[...] + 1).astype(jnp.float32)
     lane = lax.broadcasted_iota(jnp.int32, (rows, columns), 1)
     pack = jnp.zeros((rows, columns), jnp.float32)
@@ -91,22 +111,31 @@
         pack = jnp.where(place < span, value, pack)
     packed[...] = pack
 
+    load_away.wait()
+    for index in range(half):
+        bulk[index] = spectrum[other * half + index].reshape(4 * rows_all, columns).astype(jnp.bfloat16)
+    for copy in inputs[2:4]:
+        copy.wait()
+
     beside = lax.div(space + spaces - 1, spaces) + lax.div(2 * spaces - 2 - space, spaces)
     pl.semaphore_wait(barrier, count - 1 + count * beside)
 
     def halo_copy(side, step, at, slot):
         return pltpu.make_async_remote_copy(
             src_ref=packed, dst_ref=halo.at[side, slot],
-            send_sem=halo_send.at[side, step], recv_sem=halo_recv.at[side, slot],
-            device_id=device(peer(step), at), device_id_type=MESH,
+            send_sem=halo_send.at[side], recv_sem=halo_recv.at[side],
+            device_id=device(step, at), device_id_type=MESH,
         )
 
     def center_copy(step, slot):
         return pltpu.make_async_remote_copy(
             src_ref=block, dst_ref=center.at[slot],
-            send_sem=center_send.at[step], recv_sem=center_recv.at[slot],
-            device_id=device(peer(step), space), device_id_type=MESH,
-        )
+            send_sem=center_send, recv_sem=center_recv,
+            device_id=device(step, space), device_id_type=MESH,
+        )
+
+    def group_wait(buffer, semaphore):
+        pltpu.make_async_copy(buffer, buffer, semaphore).wait()
 
     partner = {"role": other, "space": space, "freq": group}
     cells_copy = pltpu.make_async_remote_copy(
@@ -137,10 +166,9 @@
     cells_copy.start()
     wavelets_copy.start()
 
-    load_away.wait()
-    for index in range(half):
-        bulk[index] = spectrum[other * half + index].reshape(4 * rows_all, columns).astype(jnp.bfloat16)
     bulk_copy.start()
+    for copy in inputs[4:]:
+        copy.wait()
 
     depth = 2 * STEPS * rows_all
     at_row = lax.broadcasted_iota(jnp.int32, (2 * rows_all, depth), 0)
@@ -176,8 +204,7 @@
     wavelets_copy.wait_recv()
     injection(1, cells_far[...], wavelets_far[0])
 
-    for step in range(1, count):
-        center_copy(step, peer(step)).wait_recv()
+    group_wait(center.at[pl.ds(0, count - 1)], center_recv)
     for plane in range(PLANES):
         center[me, plane] = block[plane]
 
@@ -189,13 +216,11 @@
 
     @pl.when(has_low)
     def _():
-        for step in range(count):
-            halo_copy(0, step, space - 1, peer(step)).wait_recv()
+        group_wait(halo.at[0], halo_recv.at[0])
 
     @pl.when(has_high)
     def _():
-        for step in range(count):
-            halo_copy(1, step, space + 1, peer(step)).wait_recv()
+        group_wait(halo.at[1], halo_recv.at[1])
 
     low_part = (lane & (span - 1)) < STEPS
     for which, owner in ((0, role), (1, other)):
@@ -295,8 +320,8 @@
     def sums_copy(step, slot):
         return pltpu.make_async_remote_copy(
             src_ref=sums.at[peer(step)], dst_ref=sums_far.at[slot],
-            send_sem=sums_send.at[step], recv_sem=sums_recv.at[slot],
-            device_id=device(peer(step), space), device_id_type=MESH,
+            send_sem=sums_send, recv_sem=sums_recv,
+            device_id=device(step, space), device_id_type=MESH,
         )
 
     for step in range(1, count):
@@ -307,35 +332,36 @@
             spectrum[other * half + index, part] = spectrum[other * half + index, part] + piece(rest, index, part)
 
     answer = sums[me]
+    group_wait(sums.at[pl.ds(0, count - 1)], sums_recv)
     for step in range(1, count):
-        sums_copy(step, peer(step)).wait_recv()
         answer = answer + sums_far[peer(step)]
     gradient[...] = answer
 
     @pl.when(has_high)
     def _():
-        for step in range(count):
-            halo_copy(0, step, space + 1, me).wait_send()
+        group_wait(halo.at[0], halo_send.at[0])
 
     @pl.when(has_low)
     def _():
-        for step in range(count):
-            halo_copy(1, step, space - 1, me).wait_send()
-
-    for step in range(1, count):
-        center_copy(step, me).wait_send()
-        sums_copy(step, me).wait_send()
+        group_wait(halo.at[1], halo_send.at[1])
+
+    group_wait(center.at[pl.ds(0, count - 1)], center_send)
+    group_wait(sums.at[pl.ds(0, count - 1)], sums_send)
     cells_copy.wait_send()
     wavelets_copy.wait_send()
     bulk_copy.wait_send()
 
 
 def deliver(fields, spectrum, gradient, fields_out, spectra_out, gradient_out, sem):
+    each = spectrum.shape[0] // PIECES
     copies = [
-        pltpu.make_async_copy(spectrum, spectra_out.at[0], sem.at[0]),
-        pltpu.make_async_copy(fields, fields_out, sem.at[1]),
-        pltpu.make_async_copy(gradient, gradient_out, sem.at[2]),
+        pltpu.make_async_copy(
+            spectrum.at[pl.ds(piece * each, each)], spectra_out.at[0, pl.ds(piece * each, each)], sem.at[piece]
+        )
+        for piece in range(PIECES)
     ]
+    copies.append(pltpu.make_async_copy(fields, fields_out, sem.at[PIECES]))
+    copies.append(pltpu.make_async_copy(gradient, gradient_out, sem.at[PIECES + 1]))
     for copy in copies:
         copy.start()
     for copy in copies:
@@ -355,7 +381,6 @@
     sizes = (groups, spaces, local_freqs, rows, columns)
     f32 = jnp.float32
     vmem = pl.BlockSpec(memory_space=pltpu.VMEM)
-    smem = pl.BlockSpec(memory_space=pltpu.SMEM)
     anywhere = pl.BlockSpec(memory_space=pl.ANY)
     dma = pltpu.SemaphoreType.DMA
     results = pl.pallas_call(
@@ -365,9 +390,15 @@
             pltpu.VMEM(spectra.shape[1:], f32),
             pltpu.VMEM((rows_all // count, columns), f32),
         ),
-        in_specs=[vmem, vmem, smem, smem, smem, vmem, vmem, anywhere],
+        in_specs=[anywhere] * 8,
         out_specs=(vmem, vmem, vmem),
         scratch_shapes=[
+            pltpu.VMEM((rows, columns), jnp.int32),
+            pltpu.SMEM((local_freqs,), jnp.int32),
+            pltpu.SMEM((local_freqs,), f32),
+            pltpu.SMEM(material.shape, f32),
+            pltpu.VMEM((1, nsrc), jnp.int32),
+            pltpu.VMEM((1, STEPS, nsrc), f32),
             pltpu.VMEM((PLANES, rows, columns), f32),
             pltpu.VMEM((rows, columns), f32),
             pltpu.VMEM((count, PLANES, rows, columns), f32),
@@ -385,8 +416,8 @@
             pltpu.VMEM((5, rows_all, columns), f32),
             pltpu.VMEM((count, rows_all // count, columns), f32),
             pltpu.VMEM((count, rows_all // count, columns), f32),
-            dma((count,)), dma((count,)), dma((2, count)), dma((2, count)), dma((2,)), dma((2,)),
-            dma, dma, dma((count,)), dma((count,)), dma((2,)),
+            dma, dma, dma((2,)), dma((2,)), dma((2,)), dma((2,)),
+            dma, dma, dma, dma, dma((2,)), dma((7,)),
         ],
         compiler_params=pltpu.CompilerParams(collective_id=0, has_side_effects=True),
     )(fields, material_ids, freq_index, freq_weight, material, source_cells, wavelets, spectra)
@@ -399,7 +430,7 @@
         ),
         in_specs=[vmem, vmem, vmem],
         out_specs=(anywhere, anywhere, anywhere),
-        scratch_shapes=[dma((3,))],
+        scratch_shapes=[dma((PIECES + 2,))],
     )(*[pltpu.with_memory_space_constraint(x, pltpu.VMEM) for x in results]))
 
 

time: 16.8 us -> 15.6 us (0.929)
  Pallas kernels: 16 us -> 14.8 us
    pallas_call x1, Pallas kernels: 15.2 us -> 13.9 us  [local(): pl.pallas_call(functools.partial(kernel, sizes), out_shape=(pltpu.VMEM(fi...]
where the time goes in v2:
time: 15.6 us; the launch traced here: 15.4 us
  Pallas kernels  14.8 us (95%)
  between operations  0.64 us (4%)
    pallas_call x1, Pallas kernels, local(): pl.pallas_call(functools.partial(kernel, sizes), out_shape=(pltpu.VMEM(fi...  13.9 us
    pallas_call x1, Pallas kernels, local(): pl.pallas_call(deliver, out_shape=(jax.ShapeDtypeStruct(fields.shape, f32...  0.87 us

profile of v2, /device:TPU:0, one launch (start us, length us, event | category | flops | bytes accessed | tf_op | source)
XLA Modules:
  0.0 15.4 jit_solution(17656660563318461986)
XLA Ops:
  0.6 13.9 %shard_map.103 = (f32[1,5,2,128]{3,2,1,0:T(2,128)S(1)}, f32[32,4,8,128]{3,2,1,0:T(8,128)S(1)}, f32[1,128]{1,0:T(1,128)S(1)}) custom-call(f32[1,5,2,128]{3,2,1,0:T(2,128)} %fields_in.1, s32[2,128]{1,0:T(2,128)} %ids_in.1, s32[32]{0:T(128)} %freq_index_in.1, f32[32]{0:T(128)} %freq_weight_in.1, f32[3,8]{1,0:T(4,128)} %material_in.1, s32[1,16]{1,0:T(1,128)} %cells_in.1, ...), custom_call_target="tpu_custom_call" | custom-call | tf_op jit(solution)/shard_map/pallas_call | solution.py:386
  14.6 0.9 %shard_map.104 = (f32[1,5,2,128]{3,2,1,0:T(2,128)}, f32[1,32,4,8,128]{4,3,2,1,0:T(8,128)}, f32[1,128]{1,0:T(1,128)}) custom-call(f32[1,5,2,128]{3,2,1,0:T(2,128)S(1)} %get-tuple-element.6.fields, f32[32,4,8,128]{3,2,1,0:T(8,128)S(1)} %get-tuple-element.7.spectrum, f32[1,128]{1,0:T(1,128)S(1)} %get-tuple-element.8.gradient), custom_call_target="tpu_custom_call" | custom-call | tf_op jit(solution)/shard_map/pallas_call | solution.py:424

commit v3 on v2

--- a/solution.py
+++ b/solution.py
@@ -13,7 +13,7 @@
 COURANT = 0.18
 TWO_PI = 6.283185307179586
 PLANES = 6
-PIECES = 8
+PIECES = 1
 MESH = pl.DeviceIdType.MESH
 
 
@@ -28,7 +28,7 @@
     fields_in, ids_in, freq_index_in, freq_weight_in, material_in, cells_in, wavelets_in, spectra,
     fields_out, spectrum, gradient,
     ids, freq_index, freq_weight, material, cells, wavelets,
-    block, packed, center, halo, cells_far, wavelets_far, planes, edges,
+    block, packed, center, halo, cells_far, wavelets_far, planes,
     inject_left, inject, table, snaps, bulk, bulk_far, final, sums, sums_far,
     center_send, center_recv, halo_send, halo_recv, small_send, small_recv,
     bulk_send, bulk_recv, sums_send, sums_recv, load_sem, input_sem,
@@ -84,13 +84,11 @@
 
     @pl.when(has_low)
     def _():
-        for step in range(count):
-            pl.semaphore_signal(barrier, inc=1, device_id=device(step, space - 1), device_id_type=MESH)
+        pl.semaphore_signal(barrier, inc=1, device_id=device(0, space - 1), device_id_type=MESH)
 
     @pl.when(has_high)
     def _():
-        for step in range(count):
-            pl.semaphore_signal(barrier, inc=1, device_id=device(step, space + 1), device_id_type=MESH)
+        pl.semaphore_signal(barrier, inc=1, device_id=device(0, space + 1), device_id_type=MESH)
 
     for step in range(1, count):
         pl.semaphore_signal(barrier, inc=1, device_id=device(step, space), device_id_type=MESH)
@@ -101,15 +99,6 @@
         copy.wait()
 
     block[PLANES - 1] = (ids[...] + 1).astype(jnp.float32)
-    lane = lax.broadcasted_iota(jnp.int32, (rows, columns), 1)
-    pack = jnp.zeros((rows, columns), jnp.float32)
-    for plane in range(PLANES):
-        value = block[plane]
-        if plane:
-            value = pltpu.roll(value, span * plane, 1)
-        place = (lane - (span * plane - STEPS)) & (columns - 1)
-        pack = jnp.where(place < span, value, pack)
-    packed[...] = pack
 
     load_away.wait()
     for index in range(half):
@@ -118,13 +107,12 @@
         copy.wait()
 
     beside = lax.div(space + spaces - 1, spaces) + lax.div(2 * spaces - 2 - space, spaces)
-    pl.semaphore_wait(barrier, count - 1 + count * beside)
-
-    def halo_copy(side, step, at, slot):
+    pl.semaphore_wait(barrier, count - 1 + beside)
+
+    def halo_copy(side, at):
         return pltpu.make_async_remote_copy(
-            src_ref=packed, dst_ref=halo.at[side, slot],
-            send_sem=halo_send.at[side], recv_sem=halo_recv.at[side],
-            device_id=device(step, at), device_id_type=MESH,
+            src_ref=packed, dst_ref=halo.at[side], send_sem=halo_send.at[side], recv_sem=halo_recv.at[side],
+            device_id=device(0, at), device_id_type=MESH,
         )
 
     def center_copy(step, slot):
@@ -150,16 +138,6 @@
         src_ref=bulk, dst_ref=bulk_far, send_sem=bulk_send, recv_sem=bulk_recv,
         device_id=partner, device_id_type=MESH,
     )
-
-    @pl.when(has_high)
-    def _():
-        for step in range(count):
-            halo_copy(0, step, space + 1, me).start()
-
-    @pl.when(has_low)
-    def _():
-        for step in range(count):
-            halo_copy(1, step, space - 1, me).start()
 
     for step in range(1, count):
         center_copy(step, me).start()
@@ -200,10 +178,6 @@
 
     injection(0, cells[...], wavelets[0])
 
-    cells_copy.wait_recv()
-    wavelets_copy.wait_recv()
-    injection(1, cells_far[...], wavelets_far[0])
-
     group_wait(center.at[pl.ds(0, count - 1)], center_recv)
     for plane in range(PLANES):
         center[me, plane] = block[plane]
@@ -214,29 +188,51 @@
             for plane in range(PLANES):
                 planes[which, plane, pl.ds(part * rows, rows), :] = center[slot, plane]
 
+    lane_all = lax.broadcasted_iota(jnp.int32, (rows_all, columns), 1)
+    for which in range(2):
+        pack = jnp.zeros((rows_all, columns), jnp.float32)
+        for plane in range(PLANES):
+            value = planes[which, plane]
+            if plane:
+                value = pltpu.roll(value, span * plane, 1)
+            place = (lane_all - (span * plane - STEPS)) & (columns - 1)
+            pack = jnp.where(place < span, value, pack)
+        packed[which] = pack
+
+    @pl.when(has_high)
+    def _():
+        halo_copy(0, space + 1).start()
+
     @pl.when(has_low)
     def _():
-        group_wait(halo.at[0], halo_recv.at[0])
-
-    @pl.when(has_high)
-    def _():
-        group_wait(halo.at[1], halo_recv.at[1])
-
-    low_part = (lane & (span - 1)) < STEPS
-    for which, owner in ((0, role), (1, other)):
-        for part in range(groups):
-            slot = owner * groups + part
-            edges[which, pl.ds(part * rows, rows), :] = jnp.where(low_part, halo[1, slot], halo[0, slot])
-
-    lane_all = lax.broadcasted_iota(jnp.int32, (rows_all, columns), 1)
+        halo_copy(1, space - 1).start()
+
     rim = (lane_all < STEPS) | (lane_all >= columns - STEPS)
 
+    low_part = (lane_all & (span - 1)) < STEPS
+
+    def outside(which):
+        return jnp.where(low_part, halo[1, which], halo[0, which])
+
     def whole(which, plane):
-        outer = edges[which]
+        outer = outer_of[which]
         if plane:
             outer = pltpu.roll(outer, columns - span * plane, 1)
         return jnp.concatenate([planes[which, plane], jnp.where(rim, outer, 0.0)], axis=1)
 
+    cells_copy.wait_recv()
+    wavelets_copy.wait_recv()
+    injection(1, cells_far[...], wavelets_far[0])
+
+    @pl.when(has_low)
+    def _():
+        group_wait(halo.at[0], halo_recv.at[0])
+
+    @pl.when(has_high)
+    def _():
+        group_wait(halo.at[1], halo_recv.at[1])
+
+    outer_of = [outside(0), outside(1)]
     ident = whole(0, PLANES - 1)
     props = [jnp.zeros_like(ident) for _ in range(3)]
     for block_id in range(nmat):
@@ -400,13 +396,12 @@
             pltpu.VMEM((1, nsrc), jnp.int32),
             pltpu.VMEM((1, STEPS, nsrc), f32),
             pltpu.VMEM((PLANES, rows, columns), f32),
-            pltpu.VMEM((rows, columns), f32),
+            pltpu.VMEM((2, rows_all, columns), f32),
             pltpu.VMEM((count, PLANES, rows, columns), f32),
-            pltpu.VMEM((2, count, rows, columns), f32),
+            pltpu.VMEM((2, 2, rows_all, columns), f32),
             pltpu.VMEM((1, nsrc), jnp.int32),
             pltpu.VMEM((1, STEPS, nsrc), f32),
             pltpu.VMEM((2, PLANES, rows_all, columns), f32),
-            pltpu.VMEM((2, rows_all, columns), f32),
             pltpu.VMEM((STEPS * rows_all, nsrc), f32),
             pltpu.VMEM((2, STEPS * rows_all, wide), f32),
             pltpu.VMEM((local_freqs * rows_all, 2 * STEPS * rows_all), jnp.bfloat16),

time: 15.6 us -> 17 us (1.090)
  Pallas kernels: 14.8 us -> 16.1 us
    pallas_call x1, Pallas kernels: 13.9 us -> 15.3 us  [local(): pl.pallas_call(functools.partial(kernel, sizes), out_shape=(pltpu.VMEM(fi...]
where the time goes in v3:
time: 17 us; the launch traced here: 16.8 us
  Pallas kernels  16.1 us (95%)
  between operations  0.64 us (4%)
    pallas_call x1, Pallas kernels, local(): pl.pallas_call(functools.partial(kernel, sizes), out_shape=(pltpu.VMEM(fi...  15.3 us
    pallas_call x1, Pallas kernels, local(): pl.pallas_call(deliver, out_shape=(jax.ShapeDtypeStruct(fields.shape, f32...  0.83 us

profile of v3, /device:TPU:0, one launch (start us, length us, event | category | flops | bytes accessed | tf_op | source)
XLA Modules:
  0.0 16.8 jit_solution(16800371306215092833)
XLA Ops:
  0.6 15.3 %shard_map.103 = (f32[1,5,2,128]{3,2,1,0:T(2,128)S(1)}, f32[32,4,8,128]{3,2,1,0:T(8,128)S(1)}, f32[1,128]{1,0:T(1,128)S(1)}) custom-call(f32[1,5,2,128]{3,2,1,0:T(2,128)} %fields_in.1, s32[2,128]{1,0:T(2,128)} %ids_in.1, s32[32]{0:T(128)} %freq_index_in.1, f32[32]{0:T(128)} %freq_weight_in.1, f32[3,8]{1,0:T(4,128)} %material_in.1, s32[1,16]{1,0:T(1,128)} %cells_in.1, ...), custom_call_target="tpu_custom_call" | custom-call | tf_op jit(solution)/shard_map/pallas_call | solution.py:382
  16.0 0.8 %shard_map.104 = (f32[1,5,2,128]{3,2,1,0:T(2,128)}, f32[1,32,4,8,128]{4,3,2,1,0:T(8,128)}, f32[1,128]{1,0:T(1,128)}) custom-call(f32[1,5,2,128]{3,2,1,0:T(2,128)S(1)} %get-tuple-element.6.fields, f32[32,4,8,128]{3,2,1,0:T(8,128)S(1)} %get-tuple-element.7.spectrum, f32[1,128]{1,0:T(1,128)S(1)} %get-tuple-element.8.gradient), custom_call_target="tpu_custom_call" | custom-call | tf_op jit(solution)/shard_map/pallas_call | solution.py:419

commit v4 on v2

--- a/solution.py
+++ b/solution.py
@@ -13,7 +13,7 @@
 COURANT = 0.18
 TWO_PI = 6.283185307179586
 PLANES = 6
-PIECES = 8
+PIECES = 1
 MESH = pl.DeviceIdType.MESH
 
 
@@ -111,9 +111,6 @@
         pack = jnp.where(place < span, value, pack)
     packed[...] = pack
 
-    load_away.wait()
-    for index in range(half):
-        bulk[index] = spectrum[other * half + index].reshape(4 * rows_all, columns).astype(jnp.bfloat16)
     for copy in inputs[2:4]:
         copy.wait()
 
@@ -166,6 +163,9 @@
     cells_copy.start()
     wavelets_copy.start()
 
+    load_away.wait()
+    for index in range(half):
+        bulk[index] = spectrum[other * half + index].reshape(4 * rows_all, columns).astype(jnp.bfloat16)
     bulk_copy.start()
     for copy in inputs[4:]:
         copy.wait()

time: 15.6 us -> 15.6 us (level)
  no operation moved by 1% of the time
where the time goes in v4:
time: 15.6 us; the launch traced here: 15.4 us
  Pallas kernels  14.7 us (94%)
  between operations  0.64 us (4%)
    pallas_call x1, Pallas kernels, local(): pl.pallas_call(functools.partial(kernel, sizes), out_shape=(pltpu.VMEM(fi...  13.9 us
    pallas_call x1, Pallas kernels, local(): pl.pallas_call(deliver, out_shape=(jax.ShapeDtypeStruct(fields.shape, f32...  0.83 us

profile of v4, /device:TPU:0, one launch (start us, length us, event | category | flops | bytes accessed | tf_op | source)
XLA Modules:
  0.0 15.4 jit_solution(5199903340195921423)
XLA Ops:
  0.6 13.9 %shard_map.103 = (f32[1,5,2,128]{3,2,1,0:T(2,128)S(1)}, f32[32,4,8,128]{3,2,1,0:T(8,128)S(1)}, f32[1,128]{1,0:T(1,128)S(1)}) custom-call(f32[1,5,2,128]{3,2,1,0:T(2,128)} %fields_in.1, s32[2,128]{1,0:T(2,128)} %ids_in.1, s32[32]{0:T(128)} %freq_index_in.1, f32[32]{0:T(128)} %freq_weight_in.1, f32[3,8]{1,0:T(4,128)} %material_in.1, s32[1,16]{1,0:T(1,128)} %cells_in.1, ...), custom_call_target="tpu_custom_call" | custom-call | tf_op jit(solution)/shard_map/pallas_call | solution.py:386
  14.6 0.8 %shard_map.104 = (f32[1,5,2,128]{3,2,1,0:T(2,128)}, f32[1,32,4,8,128]{4,3,2,1,0:T(8,128)}, f32[1,128]{1,0:T(1,128)}) custom-call(f32[1,5,2,128]{3,2,1,0:T(2,128)S(1)} %get-tuple-element.6.fields, f32[32,4,8,128]{3,2,1,0:T(8,128)S(1)} %get-tuple-element.7.spectrum, f32[1,128]{1,0:T(1,128)S(1)} %get-tuple-element.8.gradient), custom_call_target="tpu_custom_call" | custom-call | tf_op jit(solution)/shard_map/pallas_call | solution.py:424
